TPU v7x, 512 devices: a whole 4x4x16 slice. The times are simulated.
512 devices in a mesh: seq: 32 (over z, core), heads: 4 (over x), dp: 4 (over y).
Axes of the slice: x: 4, y: 4, z: 16, core: 2. Of those that a mesh axis runs over, the one named last changes fastest.
Arguments:
- tokens: bfloat16 [4, 4096, 3072], P('dp', 'seq'), may hold values from -6 to 6
- proj_weights: bfloat16 [3, 3072, 4096], P(None, 'seq', ('heads', 'dp')), may hold values from -0.109375 to 0.109375
- norm_gain: float32 [4096], P(('heads', 'dp')), may hold values from 0.5 to 1.5
Outputs:
- attended: bfloat16 [4, 4096, 4096], P('dp', 'seq', 'heads')
All inputs are finite; a program needn't handle non-finite values.
Results may differ from a plain program's by a relative error of at most 0.0063.
Values may be sent and summed in bfloat16 or wider, within the bound.
No kernel may reach another device: no remote copies, remote signals or barrier semaphores. Data moves between devices by JAX's collectives and lax.ppermute only.
A program may use at most 64 MiB of HBM per device.

v0:
```python
import jax
import jax.numpy as jnp
from jax import lax
from jax.sharding import PartitionSpec as P

DH = 128


def prefix_2(part, axis, combine, identity):
    place = lax.axis_index(axis)
    gathered = lax.all_gather(part, axis)
    state = jnp.zeros_like(part) + jnp.asarray(identity, part.dtype)

    def one(step, state):
        return combine(state, lax.dynamic_index_in_dim(gathered, step, 0, False))

    return lax.fori_loop(0, place, one, state)


def add_pair(earlier, later):
    return earlier + later


def project_rows(flat_rows):

    def accumulate(total, piece, start):
        return jnp.einsum("nd,jdc->jnc", flat_rows, piece, preferred_element_type=jnp.float32)

    return accumulate


def to_heads(matrix, seq_count, length):
    return matrix.reshape(seq_count, length, -1, DH)


def activate(matrix, seq_count, length):
    return to_heads(jax.nn.silu(matrix).astype(jnp.bfloat16), seq_count, length)


def block_prefix(keys_b, values_b):
    state = jnp.einsum("sthd,sthe->shde", keys_b, values_b, preferred_element_type=jnp.float32)
    return prefix_2(state, "seq", add_pair, jnp.zeros_like(state))


def attend(queries, keys_b, values_b, prefix, norm_gain):
    seq_count, length, head_count, head_size = queries.shape
    scores = jnp.einsum("sthd,suhd->shtu", queries, keys_b, preferred_element_type=jnp.float32)
    causal = lax.broadcasted_iota(jnp.int32, (length, length), 0) >= lax.broadcasted_iota(
        jnp.int32, (length, length), 1
    )
    scores_b = jnp.where(causal, scores, 0.0).astype(jnp.bfloat16)
    local = jnp.einsum("shtu,suhd->sthd", scores_b, values_b, preferred_element_type=jnp.float32)
    carried = jnp.einsum(
        "sthd,shde->sthe", queries, prefix.astype(jnp.bfloat16), preferred_element_type=jnp.float32
    )
    attn = local + carried
    scale = lax.rsqrt(jnp.mean(attn * attn, axis=-1, keepdims=True) + 1e-06)
    normed = attn * scale * norm_gain.reshape(head_count, head_size)
    return normed.astype(jnp.bfloat16).reshape(seq_count, length, head_count * head_size)


def body(tokens, proj_weights, norm_gain):
    everyone = lax.all_gather(tokens, "dp", axis=0, tiled=True)
    seq_count, length, width = everyone.shape
    total_rows = seq_count * length
    per_device = proj_weights.shape[2]
    accumulate = project_rows(everyone.reshape(total_rows, width))
    start_sum = jnp.zeros((3, total_rows, per_device), jnp.float32)
    projected = accumulate(
        start_sum, lax.all_gather(proj_weights, "seq", axis=1, tiled=True), jnp.int32(0)
    )
    queries = activate(projected[0], seq_count, length)
    keys_b = activate(projected[1], seq_count, length)
    values_b = to_heads(projected[2].astype(jnp.bfloat16), seq_count, length)
    prefix = block_prefix(keys_b, values_b)
    normed = attend(queries, keys_b, values_b, prefix, norm_gain)
    return lax.all_to_all(normed, "dp", split_axis=0, concat_axis=2, tiled=True)


def solution(mesh):
    in_specs = (P("dp", "seq", None), P(None, "seq", ("heads", "dp")), P(("heads", "dp")))
    out_specs = P("dp", "seq", "heads")
    return jax.shard_map(body, mesh=mesh, in_specs=in_specs, out_specs=out_specs, check_vma=False)
```

profile of v0, /device:TPU:481, one launch (start us, length us, event | category | flops | bytes accessed | tf_op | source)
XLA Modules:
  0.0 297.7 jit_solution(694654217346947341)
XLA Ops:
  6.5 0.7 all-gather.7.cloned.1.call-update
  7.3 0.7 all-gather.5.cloned.1.call-update
  8.1 47.7 %all-gather.7.cloned.1.call-done = bf16[4,128,3072]{2,1,0:T(8,128)(2,1)} async-done(((bf16[1,128,3072]{2,1,0:T(8,128)(2,1)}), bf16[4,128,3072]{2,1,0:T(8,128)(2,1)}) %all-gather.7.cloned.1.call-update) | async-done | bytes 3145744 | tf_op jit(solution)/shard_map/all_gather | solution.py:63
  55.8 76.4 %all-gather.5.cloned.1.call-done = bf16[3,3072,256]{2,1,0:T(8,128)(2,1)} async-done(((bf16[3,96,256]{2,1,0:T(8,128)(2,1)}), bf16[3,3072,256]{2,1,0:T(8,128)(2,1)}) %all-gather.5.cloned.1.call-update) | async-done | bytes 4718608 | tf_op jit(solution)/shard_map/all_gather | solution.py:70
  132.1 5.5 %convolution_bitcast_fusion = f32[3,512,256]{1,2,0:T(8,128)S(1)} fusion(bf16[3,3072,256]{2,1,0:T(8,128)(2,1)} %all-gather.5.cloned.1.call-done, bf16[512,3072,1]{1,0,2:T(8,128)(2,1)} %bitcast.33), kind=kOutput, calls=%fused_computation.1 | convolution fusion | flops 2415919104 | bytes 9437184 | tf_op jit(solution)/shard_map/nd,jdc->jnc/dot_general | solution.py:27
  137.7 0.2 squeeze.12
  137.9 0.2 copy.16
  138.2 0.2 copy.19
  138.4 1.1 fusion.7
  139.6 0.2 squeeze.11
  139.8 0.2 copy.14
  140.0 0.6 fusion.2
  140.6 101.5 %all-gather.9.cloned.1.call-done = f32[128,2,128,128]{3,2,1,0:T(8,128)} async-done(((f32[4,2,128,128]{3,2,1,0:T(8,128)}), f32[128,2,128,128]{3,2,1,0:T(8,128)}) %all-gather.9.cloned.1.call-update) | async-done | bytes 16777232 | tf_op jit(solution)/shard_map/all_gather | solution.py:11
  242.2 37.0 %while.10 = (s32[]{:T(128)}, f32[4,2,128,128]{3,2,1,0:T(8,128)S(1)}, s32[]{:T(128)}, f32[32,4,2,128,128]{4,3,2,1,0:T(8,128)}, s32[]{:T(128)}, /*index=5*/s32[]{:T(128)}, s32[]{:T(128)}) while((s32[]{:T(128)}, f32[4,2,128,128]{3,2,1,0:T(8,128)S(1)}, s32[]{:T(128)}, f32[32,4,2,128,128]{4,3,2,1,0:T(8,128)}, s32[]{:T(128)}, /*index=5*/s32[]{:T(128)}, ...), condition=%wide.region_1.2_spmd, body=%wide.region_0.1_spmd.sunk | while | flops 131077 | bytes 1572987 | solution.py:17
  242.2 1.2 bitcast_add_fusion.2
  243.4 1.2 bitcast_add_fusion.2
  244.6 1.2 bitcast_add_fusion.2
  245.8 1.2 bitcast_add_fusion.2
  247.0 1.2 bitcast_add_fusion.2
  248.2 1.2 bitcast_add_fusion.2
  249.3 1.2 bitcast_add_fusion.2
  250.5 1.2 bitcast_add_fusion.2
  251.7 1.2 bitcast_add_fusion.2
  252.9 1.2 bitcast_add_fusion.2
  254.1 1.2 bitcast_add_fusion.2
  255.3 1.2 bitcast_add_fusion.2
  256.5 1.2 bitcast_add_fusion.2
  257.7 1.2 bitcast_add_fusion.2
  258.9 1.2 bitcast_add_fusion.2
  260.1 1.2 bitcast_add_fusion.2
  261.3 1.2 bitcast_add_fusion.2
  262.5 1.2 bitcast_add_fusion.2
  263.7 1.2 bitcast_add_fusion.2
  264.9 1.2 bitcast_add_fusion.2
  266.0 1.2 bitcast_add_fusion.2
  267.2 1.2 bitcast_add_fusion.2
  268.4 1.2 bitcast_add_fusion.2
  269.6 1.2 bitcast_add_fusion.2
  270.8 1.2 bitcast_add_fusion.2
  272.0 1.2 bitcast_add_fusion.2
  273.2 1.2 bitcast_add_fusion.2
  274.4 1.2 bitcast_add_fusion.2
  275.6 1.2 bitcast_add_fusion.2
  276.8 1.2 bitcast_add_fusion.2
  278.0 1.2 bitcast_add_fusion.2
  279.2 0.4 multiply_reduce_fusion
  279.7 10.6 %all_to_all.18 = bf16[4,128,256]{1,2,0:T(8,128)(2,1)S(1)} all-to-all(bf16[4,128,256]{1,2,0:T(8,128)(2,1)S(1)} %bitcast.29), channel_id=1, replica_groups=mesh['seq'=32,'heads'=4,'dp'=4] {'dp'}, dimensions={0} | all-to-all | bytes 524288 | tf_op jit(solution)/shard_map/all_to_all | solution.py:77
  290.3 0.8 copy.24
  (13 shorter events, 0.4 us)
Async XLA Ops:
  6.5 49.2 %all-gather.7.cloned.1.call-start = ((), (), s32[]{:S(2)}) async-start(), calls=%async_computation.2 | async-start | bytes 3932160 | tf_op jit(solution)/shard_map/all_gather | solution.py:63
  7.3 124.9 %all-gather.5.cloned.1.call-start = ((), (), s32[]{:S(2)}) async-start(), calls=%async_computation.1 | async-start | bytes 4866048 | tf_op jit(solution)/shard_map/all_gather | solution.py:70
  8.0 234.1 %all-gather.9.cloned.1.call-start = ((), (), s32[]{:S(2)}) async-start(), calls=%async_computation.3 | async-start | bytes 17301504 | tf_op jit(solution)/shard_map/all_gather | solution.py:11
  242.1 37.4 %copy-start = (f32[256]{0:T(256)S(1)}, f32[256]{0:T(256)}, u32[]{:S(2)}) copy-start(f32[256]{0:T(256)} %param.7) | copy-start | bytes 3076
Sparse Core Ops, SparseCore 0:
  9.5 46.2 all-gather.6
  57.9 74.1 all-gather.4
  139.7 102.3 all-gather.8
where the time goes:
time: 299 us; the launch traced here: 298 us
  waiting for transfers between devices  227 us (76%)
  other arithmetic  36.4 us (12%)
  between operations  13.2 us (4%)
  blocking collectives  10.6 us (4%)
  matrix products  7.57 us (3%)
    all_gather x1, waiting for transfers between devices, prefix_2(): gathered = lax.all_gather(part, axis)  101 us
    all_gather x1, waiting for transfers between devices, body(): lax.all_gather(proj_weights, 'seq', axis=1, tiled=True)  76.4 us
    all_gather x1, waiting for transfers between devices, body(): everyone = lax.all_gather(tokens, 'dp', axis=0, tiled=True)  47.7 us
    add x31, other arithmetic, add_pair(): return earlier + later  36.3 us
    all_to_all x1, blocking collectives, body(): return lax.all_to_all(normed, 'dp', split_axis=0, concat_axis=2, tiled=True)  10.6 us
  transfers between devices with their start and end apart: 3, of which 3 were waited for; matrix products, arithmetic and copies ran while one was open for 0% of the time, Pallas kernels for 0%

commit v1 on v0

--- a/solution.py
+++ b/solution.py
@@ -67,7 +67,11 @@
     accumulate = project_rows(everyone.reshape(total_rows, width))
     start_sum = jnp.zeros((3, total_rows, per_device), jnp.float32)
     projected = accumulate(
-        start_sum, lax.all_gather(proj_weights, "seq", axis=1, tiled=True), jnp.int32(0)
+        start_sum,
+        jnp.concatenate(
+            lax.all_to_all(jnp.stack([proj_weights] * lax.axis_size("seq")), "seq", 0, 0), axis=1
+        ),
+        jnp.int32(0),
     )
     queries = activate(projected[0], seq_count, length)
     keys_b = activate(projected[1], seq_count, length)

time: 299 us -> 400 us (1.34)
  waiting for transfers between devices: 227 us -> 309 us
  starting transfers between devices: 0.08 us -> 9.51 us
  local copies, waits for them, and re-layouts: 2.07 us -> 10.6 us
    all_to_all x0 -> x1, waiting for transfers between devices: none -> 202 us  [body(): lax.all_to_all(jnp.stack([proj_weights] * lax.axis_size('seq')), 'seq', 0...]
    all_gather x1 -> x0, waiting for transfers between devices: 76.4 us -> none  [body(): lax.all_gather(proj_weights, 'seq', axis=1, tiled=True)]
    all_gather x1, waiting for transfers between devices: 47.7 us -> 0.01 us  [body(): everyone = lax.all_gather(tokens, 'dp', axis=0, tiled=True)]
    all_to_all x0 -> x1, starting transfers between devices: none -> 9.43 us  [body(): lax.all_to_all(jnp.stack([proj_weights] * lax.axis_size('seq')), 'seq', 0...]
    all_gather x1, waiting for transfers between devices: 101 us -> 107 us  [prefix_2(): gathered = lax.all_gather(part, axis)]
    all_to_all x0 -> x1, local copies, waits for them, and re-layouts: none -> 4.92 us  [body(): lax.all_to_all(jnp.stack([proj_weights] * lax.axis_size('seq')), 'seq', 0...]
  transfers between devices with their start and end apart: 3 -> 3, of which waited for: 3 -> 2; matrix products, arithmetic and copies ran while one was open for 0% -> 1% of each run, Pallas kernels for 0% -> 0%
where the time goes in v1:
time: 400 us; the launch traced here: 398 us
  waiting for transfers between devices  309 us (77%)
  other arithmetic  36.4 us (9%)
  between operations  13.5 us (3%)
  local copies, waits for them, and re-layouts  10.6 us (3%)
  blocking collectives  10.6 us (3%)
  starting transfers between devices  9.51 us (2%)
  matrix products  7.56 us (2%)
    all_to_all x1, waiting for transfers between devices, body(): lax.all_to_all(jnp.stack([proj_weights] * lax.axis_size('seq')), 'seq', 0...  202 us
    all_gather x1, waiting for transfers between devices, prefix_2(): gathered = lax.all_gather(part, axis)  107 us
    add x31, other arithmetic, add_pair(): return earlier + later  36.2 us
    all_to_all x1, blocking collectives, body(): return lax.all_to_all(normed, 'dp', split_axis=0, concat_axis=2, tiled=True)  10.6 us
    all_to_all x1, starting transfers between devices, body(): lax.all_to_all(jnp.stack([proj_weights] * lax.axis_size('seq')), 'seq', 0...  9.43 us
  transfers between devices with their start and end apart: 3, of which 2 were waited for; matrix products, arithmetic and copies ran while one was open for 1% of the time, Pallas kernels for 0%

profile of v1, /device:TPU:481, one launch (start us, length us, event | category | flops | bytes accessed | tf_op | source)
XLA Modules:
  0.0 398.5 jit_solution(9986925967311917879)
XLA Ops:
  6.5 3.7 stack.2
  10.2 9.4 %all-to-all-start = ((bf16[32,3,96,256]{3,2,1,0:T(8,128)(2,1)}), bf16[32,3,96,256]{3,2,1,0:T(8,128)(2,1)}, u32[]{:S(2)}, u32[]{:S(2)}) async-start(bf16[32,3,96,256]{3,2,1,0:T(8,128)(2,1)} %stack.2), calls=%async_computation | async-start | bytes 9437184 | tf_op jit(solution)/shard_map/all_to_all | solution.py:72
  19.7 0.7 all-gather.4.cloned.1.call-update
  20.4 201.8 %all-to-all-done = bf16[32,3,96,256]{3,2,1,0:T(8,128)(2,1)} async-done(((bf16[32,3,96,256]{3,2,1,0:T(8,128)(2,1)}), bf16[32,3,96,256]{3,2,1,0:T(8,128)(2,1)}, u32[]{:S(2)}, u32[]{:S(2)}) %all-to-all-start) | async-done | bytes 4718624 | tf_op jit(solution)/shard_map/all_to_all | solution.py:72
  222.2 4.9 %copy.24 = bf16[32,3,96,256]{3,2,0,1:T(8,128)(2,1)} copy(bf16[32,3,96,256]{3,2,1,0:T(8,128)(2,1)} %all-to-all-done) | data formatting | bytes 9437184 | tf_op jit(solution)/shard_map/all_to_all | solution.py:72
  227.1 5.5 %convolution_bitcast_fusion = f32[3,512,256]{1,2,0:T(8,128)S(1)} fusion(bf16[3,3072,256]{2,1,0:T(8,128)(2,1)} %bitcast.32, bf16[512,3072,1]{1,0,2:T(8,128)(2,1)} %bitcast.37), kind=kOutput, calls=%fused_computation.1 | convolution fusion | flops 2415919104 | bytes 9437184 | tf_op jit(solution)/shard_map/nd,jdc->jnc/dot_general | solution.py:27
  232.7 0.2 squeeze.12
  232.9 0.2 copy.29
  233.2 0.2 copy.32
  233.4 1.1 fusion.7
  234.8 0.2 copy.27
  235.1 0.6 fusion.2
  235.6 106.9 %all-gather.6.cloned.1.call-done = f32[128,2,128,128]{3,2,1,0:T(8,128)} async-done(((f32[4,2,128,128]{3,2,1,0:T(8,128)}), f32[128,2,128,128]{3,2,1,0:T(8,128)}) %all-gather.6.cloned.1.call-update) | async-done | bytes 16777232 | tf_op jit(solution)/shard_map/all_gather | solution.py:11
  342.6 37.1 %while.10 = (s32[]{:T(128)}, f32[4,2,128,128]{3,2,1,0:T(8,128)S(1)}, s32[]{:T(128)}, f32[32,4,2,128,128]{4,3,2,1,0:T(8,128)}, s32[]{:T(128)}, /*index=5*/s32[]{:T(128)}, s32[]{:T(128)}) while((s32[]{:T(128)}, f32[4,2,128,128]{3,2,1,0:T(8,128)S(1)}, s32[]{:T(128)}, f32[32,4,2,128,128]{4,3,2,1,0:T(8,128)}, s32[]{:T(128)}, /*index=5*/s32[]{:T(128)}, ...), condition=%wide.region_1.2_spmd, body=%wide.region_0.1_spmd.sunk | while | flops 131077 | bytes 1572979 | solution.py:17
  342.6 1.2 bitcast_add_fusion.2
  343.8 1.2 bitcast_add_fusion.2
  345.0 1.2 bitcast_add_fusion.2
  346.2 1.2 bitcast_add_fusion.2
  347.4 1.2 bitcast_add_fusion.2
  348.6 1.2 bitcast_add_fusion.2
  349.8 1.2 bitcast_add_fusion.2
  351.0 1.2 bitcast_add_fusion.2
  352.1 1.2 bitcast_add_fusion.2
  353.3 1.2 bitcast_add_fusion.2
  354.5 1.2 bitcast_add_fusion.2
  355.7 1.2 bitcast_add_fusion.2
  356.9 1.2 bitcast_add_fusion.2
  358.1 1.2 bitcast_add_fusion.2
  359.3 1.2 bitcast_add_fusion.2
  360.5 1.2 bitcast_add_fusion.2
  361.7 1.2 bitcast_add_fusion.2
  362.9 1.2 bitcast_add_fusion.2
  364.1 1.2 bitcast_add_fusion.2
  365.3 1.2 bitcast_add_fusion.2
  366.5 1.2 bitcast_add_fusion.2
  367.7 1.2 bitcast_add_fusion.2
  368.9 1.2 bitcast_add_fusion.2
  370.1 1.2 bitcast_add_fusion.2
  371.3 1.2 bitcast_add_fusion.2
  372.5 1.2 bitcast_add_fusion.2
  373.7 1.2 bitcast_add_fusion.2
  374.9 1.2 bitcast_add_fusion.2
  376.1 1.2 bitcast_add_fusion.2
  377.3 1.2 bitcast_add_fusion.2
  378.5 1.2 bitcast_add_fusion.2
  379.7 0.4 multiply_reduce_fusion
  380.1 10.6 %all_to_all.23 = bf16[4,128,256]{1,2,0:T(8,128)(2,1)S(1)} all-to-all(bf16[4,128,256]{1,2,0:T(8,128)(2,1)S(1)} %bitcast.33), channel_id=1, replica_groups=mesh['seq'=32,'heads'=4,'dp'=4] {'dp'}, dimensions={0} | all-to-all | bytes 524288 | tf_op jit(solution)/shard_map/all_to_all | solution.py:81
  390.8 0.8 copy.38
  (14 shorter events, 0.6 us)
Async XLA Ops:
  10.2 212.0 %all-to-all-start = ((bf16[32,3,96,256]{3,2,1,0:T(8,128)(2,1)}), bf16[32,3,96,256]{3,2,1,0:T(8,128)(2,1)}, u32[]{:S(2)}, u32[]{:S(2)}) async-start(bf16[32,3,96,256]{3,2,1,0:T(8,128)(2,1)} %stack.2), calls=%async_computation | async-start | bytes 9437184 | tf_op jit(solution)/shard_map/all_to_all | solution.py:72
  19.6 207.5 %all-gather.4.cloned.1.call-start = ((), (), s32[]{:S(2)}) async-start(), calls=%async_computation.2 | async-start | bytes 3932160 | tf_op jit(solution)/shard_map/all_gather | solution.py:63
  20.4 322.1 %all-gather.6.cloned.1.call-start = ((), (), s32[]{:S(2)}) async-start(), calls=%async_computation.3 | async-start | bytes 17301504 | tf_op jit(solution)/shard_map/all_gather | solution.py:11
  342.5 37.5 %copy-start = (f32[256]{0:T(256)S(1)}, f32[256]{0:T(256)}, u32[]{:S(2)}) copy-start(f32[256]{0:T(256)} %param.7) | copy-start | bytes 3076
Sparse Core Ops, SparseCore 0:
  22.6 49.0 all-gather.3
  234.7 107.7 all-gather.5
